TPU v7x, 32 devices: a whole 2x2x4 slice. The times are simulated.
32 devices in a mesh: layer: 2 (over x), row: 4 (over z), col: 4 (over y, core).
Axes of the slice: x: 2, y: 2, z: 4, core: 2. Of those that a mesh axis runs over, the one named last changes fastest.
Arguments:
- query_weight: bfloat16 [32768, 16384], P(('layer', 'row'), 'col'), parts along dimension 0, may hold values from -0.046875 to 0.046875
- sign_input: int32 [32768], P(('layer', 'col')), parts along dimension 0, may hold values from -1 to 1, as said below
- sign_output: int32 [32768], P(('layer', 'row')), parts along dimension 0, may hold values from -1 to 1, as said below
- clip_level: int32 [256, 128], P(('layer', 'row'), 'col'), parts along dimension 0, may hold values from 1 to 8
- calibration: bfloat16 [768, 16384], P(('layer', 'row'), 'col'), parts along dimension 0, may hold values from -6 to 6
Outputs:
- projected: bfloat16 [768, 16384], P(('layer', 'col'), 'row'), parts along dimension 0
There are 2 independent parts, one for each index of `layer`. A program takes and returns all parts, laid end to end along the dimension named above; each array names one. Nothing has to cross between parts.
Inputs may be any that keep to these rules, and one draw needn't show every extreme that they name: `sign_input`: every entry is -1 or 1. `sign_output`: every entry is -1 or 1.
All inputs are finite; a program needn't handle non-finite values.
Results may differ from a plain program's by a relative error of at most 0.0064.
Values may be sent and summed in bfloat16 or wider, within the bound.
A program may use at most 256 MiB of HBM per device.

v0:
```python
import functools

import jax
import jax.numpy as jnp
from jax import lax
from jax.experimental import pallas as pl
from jax.experimental.pallas import tpu as pltpu
from jax.sharding import PartitionSpec as P

INNER = 1024
D = 16384
BLK = 128
LANES = 128


def sylvester_bf16(length):
    at = jnp.arange(length, dtype=jnp.int32)
    parity = lax.population_count(at[:, None] & at[None, :]) & 1
    return (1 - 2 * parity).astype(jnp.bfloat16)


def inner_kernel(pieces, piece_rows, step, w_ref, si_ref, so_ref, k_ref, out_ref, ws_ref, ks_ref):
    ws_ref[...] = (w_ref[...].astype(jnp.float32) * si_ref[...]).astype(jnp.bfloat16)
    ks_ref[...] = (k_ref[...].astype(jnp.float32) * so_ref[0]).astype(jnp.bfloat16)
    inner = ws_ref.shape[0]

    @pl.loop(0, inner // step)
    def _(n):
        cols = pl.ds(pl.multiple_of(n * step, step), step)
        right = jnp.dot(ws_ref[...], k_ref[:, cols], preferred_element_type=jnp.float32)
        both = jnp.dot(ks_ref[...], right.astype(jnp.bfloat16), preferred_element_type=jnp.float32)
        out_ref[:, 0, :, cols] = both.reshape(pieces, piece_rows, step).astype(jnp.bfloat16)


def inner_both(weight, signs_in, signs_out, table, block, pieces):
    inner = table.shape[0]
    out_blocks = weight.shape[0] // inner
    piece_rows = inner // pieces
    step = min(256, inner)
    return pl.pallas_call(
        functools.partial(inner_kernel, pieces, piece_rows, step),
        grid=(out_blocks,),
        in_specs=[
            pl.BlockSpec((inner, inner), lambda c: (c, block)),
            pl.BlockSpec((1, inner), lambda c: (0, block)),
            pl.BlockSpec((1, 1, inner), lambda c: (c, 0, 0)),
            pl.BlockSpec((inner, inner), lambda c: (0, 0)),
        ],
        out_specs=pl.BlockSpec((pieces, 1, piece_rows, inner), lambda c: (0, c, 0, 0)),
        out_shape=jax.ShapeDtypeStruct((pieces, out_blocks, piece_rows, inner), jnp.bfloat16),
        scratch_shapes=[pltpu.VMEM((inner, inner), jnp.bfloat16)] * 2,
        cost_estimate=pl.CostEstimate(
            flops=4 * out_blocks * inner**3, bytes_accessed=4 * out_blocks * inner**2, transcendentals=0
        ),
    )(weight, signs_in, signs_out, table)


def butterfly(values):
    values = list(values)
    half = 1
    while half < len(values):
        for at in range(len(values)):
            if not at & half:
                low, high = values[at], values[at + half]
                values[at], values[at + half] = low + high, low - high
        half *= 2
    return values


def outer_kernel(row_count, col_count, out_blocks, in_blocks, scale, level_ref, *refs):
    parts = refs[:in_blocks]
    cal_ref, out_ref, mix_ref, clip_ref = refs[in_blocks:]
    b_at, d_at = pl.program_id(0), pl.program_id(1)
    chunk = mix_ref.shape[-1]
    lane_steps = chunk // LANES
    outer_rows = row_count * out_blocks
    outer_cols = col_count * in_blocks
    lane_blocks = level_ref.shape[1] // outer_cols

    @pl.loop(0, col_count * lane_steps)
    def _(at):
        q, lane = at // lane_steps, lax.rem(at, lane_steps)
        cols = pl.ds(pl.multiple_of(lane * LANES, LANES), LANES)
        for k in range(in_blocks):
            mixed = butterfly(
                parts[k][t * col_count + q, j, :, cols].astype(jnp.float32)
                for t in range(row_count)
                for j in range(out_blocks)
            )
            for o in range(outer_rows):
                mix_ref[q * in_blocks + k, o, :, cols] = mixed[o]

    @pl.loop(0, outer_rows * lane_steps)
    def _(at):
        o, lane = at // lane_steps, lax.rem(at, lane_steps)
        cols = pl.ds(pl.multiple_of(lane * LANES, LANES), LANES)
        mixed = butterfly(mix_ref[i, o, :, cols] for i in range(outer_cols))
        for i in range(outer_cols):
            level = level_ref[o, i * lane_blocks + b_at * lane_steps + lane]
            limit = level.astype(jnp.float32) / 512.0
            rotated = mixed[i] * scale
            clip_ref[i, o, :, cols] = jnp.minimum(jnp.maximum(rotated, -limit), limit).astype(jnp.bfloat16)

    total = None
    rows = clip_ref.shape[1] * clip_ref.shape[2]
    for q in range(col_count):
        for k in range(in_blocks):
            cal = cal_ref[:, q, k]
            cal = cal.reshape(cal.shape[0] * cal.shape[1], chunk)
            term = lax.dot_general(
                cal,
                clip_ref[q * in_blocks + k].reshape(rows, chunk),
                (((1,), (1,)), ((), ())),
                preferred_element_type=jnp.float32,
            )
            total = term if total is None else total + term

    @pl.when(b_at == 0)
    def _():
        out_ref[d_at] = total

    @pl.when(b_at > 0)
    def _():
        out_ref[d_at] += total


def outer_project(parts, level, cal, row_count, col_count, scale):
    in_blocks = len(parts)
    pieces, out_blocks, piece_rows, inner = parts[0].shape
    d_block = min(16, piece_rows)
    chunk = min(256, inner)
    outer_rows, outer_cols = row_count * out_blocks, col_count * in_blocks
    cal_local = cal.shape[3]
    cal_rows = row_count * cal_local
    d_steps = piece_rows // d_block
    return pl.pallas_call(
        functools.partial(outer_kernel, row_count, col_count, out_blocks, in_blocks, scale),
        grid=(inner // chunk, d_steps),
        in_specs=[pl.BlockSpec(memory_space=pltpu.SMEM)]
        + [pl.BlockSpec((pieces, out_blocks, d_block, chunk), lambda b, d: (0, 0, d, b))] * in_blocks
        + [pl.BlockSpec((row_count, col_count, in_blocks, cal_local, chunk), lambda b, d: (0, 0, 0, 0, b))],
        out_specs=pl.BlockSpec((d_steps, cal_rows, outer_rows * d_block), lambda b, d: (0, 0, 0)),
        out_shape=jax.ShapeDtypeStruct((d_steps, cal_rows, outer_rows * d_block), jnp.float32),
        scratch_shapes=[
            pltpu.VMEM((outer_cols, outer_rows, d_block, chunk), jnp.float32),
            pltpu.VMEM((outer_cols, outer_rows, d_block, chunk), jnp.bfloat16),
        ],
    )(level, *parts, cal)


def shards(query_weight, sign_input, sign_output, clip_level, calibration):
    rows_local, cols_local = query_weight.shape
    row_count = lax.axis_size("row")
    col_count = lax.axis_size("col")
    pieces = row_count * col_count
    out_blocks = rows_local // INNER
    in_blocks = cols_local // INNER
    piece_rows = INNER // pieces
    cal_local = calibration.shape[0]
    axes = ("row", "col")

    cal = calibration.reshape(cal_local, in_blocks, INNER).transpose(1, 0, 2)
    cal = lax.all_gather(cal, axes, axis=0, tiled=False)
    cal = cal.reshape(row_count, col_count, in_blocks, cal_local, INNER)
    level = lax.all_gather(lax.all_gather(clip_level, "col", axis=1, tiled=True), "row", axis=0, tiled=True)
    place = lax.axis_index("row") * col_count + lax.axis_index("col")
    level = level.reshape(row_count * out_blocks, INNER // BLK, -1)
    level = lax.dynamic_index_in_dim(level, place * piece_rows // BLK, axis=1, keepdims=False)

    table = sylvester_bf16(INNER)
    signs_in = sign_input.astype(jnp.float32).reshape(1, cols_local)
    signs_out = sign_output.astype(jnp.float32).reshape(out_blocks, 1, INNER)
    parts = []
    for block in range(in_blocks):
        tile = inner_both(query_weight, signs_in, signs_out, table, block, pieces)
        parts.append(lax.all_to_all(tile, axes, split_axis=0, concat_axis=0, tiled=True))

    total = outer_project(parts, level, cal, row_count, col_count, 1.0 / D)
    d_steps, cal_rows = total.shape[:2]
    d_block = piece_rows // d_steps
    result = total.astype(jnp.bfloat16)
    result = result.reshape(d_steps, col_count, cal_rows // col_count, row_count, out_blocks, d_block)
    result = result.transpose(3, 1, 2, 4, 0, 5)
    result = result.reshape(pieces, cal_rows // col_count, out_blocks, piece_rows)
    result = lax.all_to_all(result, axes, split_axis=0, concat_axis=0, tiled=True)
    return result.transpose(1, 2, 0, 3).reshape(cal_rows // col_count, rows_local)


def solution(mesh):
    placed = (
        P(("layer", "row"), "col"),
        P(("layer", "col")),
        P(("layer", "row")),
        P(("layer", "row"), "col"),
        P(("layer", "row"), "col"),
    )
    return jax.shard_map(
        shards, mesh=mesh, in_specs=placed, out_specs=P(("layer", "col"), "row"), check_vma=False
    )
```

profile of v0, /device:TPU:0, one launch (start us, length us, event | category | flops | bytes accessed | tf_op | source)
XLA Modules:
  0.0 997.0 jit_solution(11558885438403139765)
XLA Ops:
  6.5 2.5 subtract_convert_fusion.k_ref
  9.0 1.3 convert_element_type.18
  10.4 1.3 convert_element_type.19
  11.7 42.7 %shard_map.55 = bf16[16,4,64,1024]{3,2,1,0:T(8,128)(2,1)} custom-call(bf16[4096,4096]{1,0:T(8,128)(2,1)} %w_ref.7, f32[1,4096]{1,0:T(1,128)} %bitcast.20, f32[4,1,1024]{2,1,0:T(1,128)} %bitcast.24, bf16[1024,1024]{1,0:T(8,128)(2,1)} %subtract_convert_fusion.k_ref), custom_call_target="tpu_custom_call" | custom-call | flops 17179869184 | bytes 16777216 | tf_op jit(solution)/shard_map/pallas_call | solution.py:40
  54.4 7.4 all-to-all-start
  61.8 42.8 %shard_map.56 = bf16[16,4,64,1024]{3,2,1,0:T(8,128)(2,1)} custom-call(bf16[4096,4096]{1,0:T(8,128)(2,1)} %w_ref.7, f32[1,4096]{1,0:T(1,128)} %bitcast.21, f32[4,1,1024]{2,1,0:T(1,128)} %bitcast.25, bf16[1024,1024]{1,0:T(8,128)(2,1)} %subtract_convert_fusion.k_ref), custom_call_target="tpu_custom_call" | custom-call | flops 17179869184 | bytes 16777216 | tf_op jit(solution)/shard_map/pallas_call | solution.py:40
  104.7 107.9 %all-to-all-done.refs_0_ = bf16[16,4,64,1024]{3,2,1,0:T(8,128)(2,1)} async-done(((bf16[16,4,64,1024]{3,2,1,0:T(8,128)(2,1)}), bf16[16,4,64,1024]{3,2,1,0:T(8,128)(2,1)}, u32[]{:S(2)}, u32[]{:S(2)}) %all-to-all-start) | async-done | bytes 8388640 | tf_op jit(solution)/shard_map/all_to_all | solution.py:176
  212.5 36.5 %all-to-all-start.1 = ((bf16[16,4,64,1024]{3,2,1,0:T(8,128)(2,1)}), bf16[16,4,64,1024]{3,2,1,0:T(8,128)(2,1)}, u32[]{:S(2)}, u32[]{:S(2)}) async-start(bf16[16,4,64,1024]{3,2,1,0:T(8,128)(2,1)} %shard_map.56), calls=%async_computation.1 | async-start | bytes 16777216 | tf_op jit(solution)/shard_map/all_to_all | solution.py:176
  249.1 42.7 %shard_map.57 = bf16[16,4,64,1024]{3,2,1,0:T(8,128)(2,1)} custom-call(bf16[4096,4096]{1,0:T(8,128)(2,1)} %w_ref.7, f32[1,4096]{1,0:T(1,128)} %bitcast.22, f32[4,1,1024]{2,1,0:T(1,128)} %bitcast.26, bf16[1024,1024]{1,0:T(8,128)(2,1)} %subtract_convert_fusion.k_ref), custom_call_target="tpu_custom_call" | custom-call | flops 17179869184 | bytes 16777216 | tf_op jit(solution)/shard_map/pallas_call | solution.py:40
  291.8 0.0 copy-start
  291.8 108.0 %all-to-all-done.1.refs_1_ = bf16[16,4,64,1024]{3,2,1,0:T(8,128)(2,1)} async-done(((bf16[16,4,64,1024]{3,2,1,0:T(8,128)(2,1)}), bf16[16,4,64,1024]{3,2,1,0:T(8,128)(2,1)}, u32[]{:S(2)}, u32[]{:S(2)}) %all-to-all-start.1) | async-done | bytes 8388640 | tf_op jit(solution)/shard_map/all_to_all | solution.py:176
  399.8 36.5 %all-to-all-start.2 = ((bf16[16,4,64,1024]{3,2,1,0:T(8,128)(2,1)}), bf16[16,4,64,1024]{3,2,1,0:T(8,128)(2,1)}, u32[]{:S(2)}, u32[]{:S(2)}) async-start(bf16[16,4,64,1024]{3,2,1,0:T(8,128)(2,1)} %shard_map.57), calls=%async_computation.2 | async-start | bytes 16777216 | tf_op jit(solution)/shard_map/all_to_all | solution.py:176
  436.4 0.0 all-gather.3.cloned.1.call-start
  436.4 0.0 copy-done
  436.4 0.6 reshape.27
  437.0 1.1 copy.22
  438.1 0.0 all-gather.3.cloned.1.call-update
  438.1 42.8 %shard_map.58 = bf16[16,4,64,1024]{3,2,1,0:T(8,128)(2,1)} custom-call(bf16[4096,4096]{1,0:T(8,128)(2,1)} %w_ref.7, f32[1,4096]{1,0:T(1,128)} %bitcast.23, f32[4,1,1024]{2,1,0:T(1,128)} %bitcast.27, bf16[1024,1024]{1,0:T(8,128)(2,1)} %subtract_convert_fusion.k_ref), custom_call_target="tpu_custom_call" | custom-call | flops 17179869184 | bytes 16777216 | tf_op jit(solution)/shard_map/pallas_call | solution.py:40
  480.9 0.0 copy-start.1
  480.9 182.1 %all-to-all-done.2.refs_2_ = bf16[16,4,64,1024]{3,2,1,0:T(8,128)(2,1)} async-done(((bf16[16,4,64,1024]{3,2,1,0:T(8,128)(2,1)}), bf16[16,4,64,1024]{3,2,1,0:T(8,128)(2,1)}, u32[]{:S(2)}, u32[]{:S(2)}) %all-to-all-start.2) | async-done | bytes 8388640 | tf_op jit(solution)/shard_map/all_to_all | solution.py:176
  662.9 36.5 %all-to-all-start.3 = ((bf16[16,4,64,1024]{3,2,1,0:T(8,128)(2,1)}), bf16[16,4,64,1024]{3,2,1,0:T(8,128)(2,1)}, u32[]{:S(2)}, u32[]{:S(2)}) async-start(bf16[16,4,64,1024]{3,2,1,0:T(8,128)(2,1)} %shard_map.58), calls=%async_computation.3 | async-start | bytes 16777216 | tf_op jit(solution)/shard_map/all_to_all | solution.py:176
  699.4 0.0 copy-done.1
  699.4 0.1 copy.20
  699.5 38.9 %all_gather.12 = s32[32,128]{0,1:T(8,128)S(1)} all-gather(s32[32,32]{0,1:T(8,128)S(1)} %copy.20), channel_id=1, replica_groups=mesh['layer'=2,'row'=4,'col'=4] {'col'}, dimensions={1}, use_global_device_ids=true | all-gather | bytes 20480 | tf_op jit(solution)/shard_map/all_gather | solution.py:165
  738.4 0.1 copy.21
  738.5 150.6 %all_gather.13 = s32[128,128]{1,0:T(8,128)S(1)} all-gather(s32[32,128]{1,0:T(8,128)S(1)} %copy.21), channel_id=1, replica_groups=mesh['layer'=2,'row'=4,'col'=4] {'row'}, dimensions={0}, use_global_device_ids=true | all-gather | bytes 81920 | tf_op jit(solution)/shard_map/all_gather | solution.py:165
  889.0 0.6 constant_dynamic-slice_fusion
  889.6 0.0 all-to-all-done.3.refs_3_
  889.6 0.0 all-gather.3.cloned.1.call-done
  889.6 67.1 %shard_map.59 = f32[4,384,256]{2,1,0:T(8,128)} custom-call(s32[16,128]{1,0:T(8,128)} %bitcast.19, bf16[16,4,64,1024]{3,2,1,0:T(8,128)(2,1)} %all-to-all-done.refs_0_, bf16[16,4,64,1024]{3,2,1,0:T(8,128)(2,1)} %all-to-all-done.1.refs_1_, bf16[16,4,64,1024]{3,2,1,0:T(8,128)(2,1)} %all-to-all-done.2.refs_2_, bf16[16,4,64,1024]{3,2,1,0:T(8,128)(2,1)} %all-to-all-done.3.refs_3_, ...), custom_call_target="tpu_custom_call" | custom-call | tf_op jit(solution)/shard_map/pallas_call | solution.py:136
  956.7 1.5 convert_element_type.21
  958.2 0.4 copy.23
  958.6 0.6 reshape.29
  959.2 0.3 copy.24
  959.5 29.3 %all_to_all.25 = bf16[16,96,4,64]{1,3,2,0:T(8,128)(2,1)S(1)} all-to-all(bf16[16,96,4,64]{1,3,2,0:T(8,128)(2,1)S(1)} %bitcast.15), channel_id=1, replica_groups=mesh['layer'=2,'row'=4,'col'=4] {'row','col'}, dimensions={0} | all-to-all | bytes 1572864 | tf_op jit(solution)/shard_map/all_to_all | solution.py:185
  988.8 0.1 copy.25
  988.9 1.2 copy.26
Async XLA Ops:
  54.4 158.2 %all-to-all-start = ((bf16[16,4,64,1024]{3,2,1,0:T(8,128)(2,1)}), bf16[16,4,64,1024]{3,2,1,0:T(8,128)(2,1)}, u32[]{:S(2)}, u32[]{:S(2)}) async-start(bf16[16,4,64,1024]{3,2,1,0:T(8,128)(2,1)} %shard_map.55), calls=%async_computation | async-start | bytes 16777216 | tf_op jit(solution)/shard_map/all_to_all | solution.py:176
  212.5 187.3 %all-to-all-start.1 = ((bf16[16,4,64,1024]{3,2,1,0:T(8,128)(2,1)}), bf16[16,4,64,1024]{3,2,1,0:T(8,128)(2,1)}, u32[]{:S(2)}, u32[]{:S(2)}) async-start(bf16[16,4,64,1024]{3,2,1,0:T(8,128)(2,1)} %shard_map.56), calls=%async_computation.1 | async-start | bytes 16777216 | tf_op jit(solution)/shard_map/all_to_all | solution.py:176
  291.8 144.6 %copy-start = (bf16[96,4096]{1,0:T(8,128)(2,1)S(1)}, bf16[96,4096]{1,0:T(8,128)(2,1)}, u32[]{:S(2)}) copy-start(bf16[96,4096]{1,0:T(8,128)(2,1)} %param.9) | copy-start | bytes 2359300
  399.8 263.1 %all-to-all-start.2 = ((bf16[16,4,64,1024]{3,2,1,0:T(8,128)(2,1)}), bf16[16,4,64,1024]{3,2,1,0:T(8,128)(2,1)}, u32[]{:S(2)}, u32[]{:S(2)}) async-start(bf16[16,4,64,1024]{3,2,1,0:T(8,128)(2,1)} %shard_map.57), calls=%async_computation.2 | async-start | bytes 16777216 | tf_op jit(solution)/shard_map/all_to_all | solution.py:176
  436.4 453.3 %all-gather.3.cloned.1.call-start = ((), (), s32[]{:S(2)}) async-start(), calls=%async_computation.5 | async-start | bytes 13369344 | tf_op jit(solution)/shard_map/all_gather | solution.py:163
  480.9 218.5 %copy-start.1 = (s32[32,32]{1,0:T(8,128)S(1)}, s32[32,32]{1,0:T(8,128)}, u32[]{:S(2)}) copy-start(s32[32,32]{1,0:T(8,128)} %param.8) | copy-start | bytes 12292
  662.9 226.7 %all-to-all-start.3 = ((bf16[16,4,64,1024]{3,2,1,0:T(8,128)(2,1)}), bf16[16,4,64,1024]{3,2,1,0:T(8,128)(2,1)}, u32[]{:S(2)}, u32[]{:S(2)}) async-start(bf16[16,4,64,1024]{3,2,1,0:T(8,128)(2,1)} %shard_map.58), calls=%async_computation.3 | async-start | bytes 16777216 | tf_op jit(solution)/shard_map/all_to_all | solution.py:176
Sparse Core Ops, SparseCore 0:
  439.5 217.6 all-gather.2
where the time goes:
time: 998 us; the launch traced here: 997 us
  waiting for transfers between devices  398 us (40%)
  Pallas kernels  238 us (24%)
  blocking collectives  219 us (22%)
  starting transfers between devices  117 us (12%)
  between operations  13.5 us (1%)
    all_to_all x4, waiting for transfers between devices, shards(): lax.all_to_all(tile, axes, split_axis=0, concat_axis=0, tiled=True)  398 us
    pallas_call x4, Pallas kernels, inner_both(): pl.pallas_call(functools.partial(inner_kernel, pieces, piece_rows, step),...  171 us
    all_gather x1, blocking collectives, shards(): lax.all_gather(lax.all_gather(clip_level, 'col', axis=1, tiled=True), 'ro...  151 us
    all_to_all x4, starting transfers between devices, shards(): lax.all_to_all(tile, axes, split_axis=0, concat_axis=0, tiled=True)  117 us
    pallas_call x1, Pallas kernels, outer_project(): pl.pallas_call(functools.partial(outer_kernel, row_count, col_count, out_...  67.1 us
    all_gather x1, blocking collectives, shards(): lax.all_gather(clip_level, 'col', axis=1, tiled=True)  38.9 us
    all_to_all x1, blocking collectives, shards(): lax.all_to_all(result, axes, split_axis=0, concat_axis=0, tiled=True)  29.3 us
  transfers between devices with their start and end apart: 5, of which 3 were waited for; matrix products, arithmetic and copies ran while one was open for 0% of the time, Pallas kernels for 13%

commit v1 on v0

v1 whole, which is shorter than its diff:
```python
import functools

import jax
import jax.numpy as jnp
from jax import lax
from jax.experimental import pallas as pl
from jax.experimental.pallas import tpu as pltpu
from jax.sharding import PartitionSpec as P

INNER = 1024
D = 16384
BLK = 128
LEVEL_UNIT = 512
GROUP = 256
SEND_SLOTS = 3
WEIGHT_SLOTS = 3
MESH = pl.DeviceIdType.MESH


def bits_of(size):
    bits = []
    while size > 1:
        size //= 2
        bits.append(size)
    return bits


def flip(at, bit):
    return at + bit * (1 - 2 * lax.rem(at // bit, 2))


def exclusive_or(a, b, size):
    total = 0
    for bit in bits_of(size):
        total = total + bit * lax.rem(a // bit + b // bit, 2)
    return total


def sylvester(size):
    x = lax.broadcasted_iota(jnp.int32, (size, size), 0) & lax.broadcasted_iota(jnp.int32, (size, size), 1)
    x = x ^ (x >> 4)
    x = x ^ (x >> 2)
    x = x ^ (x >> 1)
    return (1 - 2 * (x & 1)).astype(jnp.float32)


def butterfly(values):
    values = list(values)
    half = 1
    while half < len(values):
        for at in range(len(values)):
            if not at & half:
                low, high = values[at], values[at + half]
                values[at], values[at + half] = low + high, low - high
        half *= 2
    return values


def kernel(
    R, C, w_ref, si_ref, so_ref, level_ref, cal_ref, recv_ref, out_ref,
    kout, skin, kin, wbuf, right, sbuf, rbuf, mix, clip, acc, accb, perm, calv, levv, levb, lim, ostage,
    wsem, ssem, own_sem, rsem, usem, cal_own, cal_send, cal_recv, lev_send, lev_recv, out_send, out_recv,
):
    layer, r, c = lax.axis_index("layer"), lax.axis_index("row"), lax.axis_index("col")
    n = R * C
    me = r * C + c
    units, _, ob, ds, wide = recv_ref.shape
    ib = wide // BLK
    chunks = INNER // BLK
    S = units // chunks
    pr = S * ds
    ao, ai = R * ob, C * ib
    groups = INNER // BLK
    blocks = ob * ib
    lev_cols = level_ref.shape[1]
    row_bits, col_bits = bits_of(R), bits_of(C)
    stages = len(row_bits) + len(col_bits)

    def peer(i):
        pr_, pc_ = exclusive_or(r, i // C, R), exclusive_or(c, lax.rem(i, C), C)
        return (layer, pr_, pc_), pr_ * C + pc_

    def w_copy(q):
        block, slot = lax.rem(q, blocks), lax.rem(q, WEIGHT_SLOTS)
        rows = pl.ds(pl.multiple_of((block // ib) * INNER, INNER), INNER)
        cols = pl.ds(pl.multiple_of(lax.rem(block, ib) * INNER, INNER), INNER)
        return pltpu.make_async_copy(w_ref.at[rows, cols], wbuf.at[slot], wsem.at[slot])

    def cal_slot(rr, cc):
        slot, weight = 0, 1
        for bit in row_bits:
            slot = slot + weight * lax.rem(r // bit + rr // bit, 2)
            weight *= 2
        for bit in col_bits:
            slot = slot + weight * lax.rem(c // bit + cc // bit, 2)
            weight *= 2
        return slot

    def cal_copy(stage):
        size = 2**stage
        if stage < len(row_bits):
            target = (layer, flip(r, row_bits[stage]), c)
        else:
            target = (layer, r, flip(c, col_bits[stage - len(row_bits)]))
        return pltpu.make_async_remote_copy(
            src_ref=cal_ref if stage == 0 else calv.at[pl.ds(0, size)],
            dst_ref=calv.at[1] if stage == 0 else calv.at[pl.ds(size, size)],
            send_sem=cal_send.at[stage],
            recv_sem=cal_recv.at[stage],
            device_id=target,
            device_id_type=MESH,
        )

    cal_own_copy = pltpu.make_async_copy(cal_ref, calv.at[0], cal_own)

    def cal_advance(stage):
        if stage >= stages:
            return
        if stage == 0:
            cal_own_copy.wait()
        cal_copy(stage).wait_recv()
        if stage + 1 < stages:
            cal_copy(stage + 1).start()

    barrier = pltpu.get_barrier_semaphore()

    @pl.loop(1, n)
    def _(i):
        target, _ = peer(i)
        pl.semaphore_signal(barrier, inc=1, device_id=target, device_id_type=MESH)

    cal_own_copy.start()
    for q in range(WEIGHT_SLOTS - 1):
        w_copy(q).start()
    pl.semaphore_wait(barrier, n - 1)

    if stages:
        cal_copy(0).start()
    pltpu.make_async_copy(level_ref, levv.at[me], lev_recv).start()

    @pl.loop(1, n)
    def _(i):
        target, _ = peer(i)
        pltpu.make_async_remote_copy(
            src_ref=level_ref, dst_ref=levv.at[me], send_sem=lev_send, recv_sem=lev_recv,
            device_id=target, device_id_type=MESH,
        ).start()

    table = sylvester(BLK)
    table_b = table.astype(jnp.bfloat16)
    diagonal = lax.broadcasted_iota(jnp.int32, (BLK, BLK), 0) == lax.broadcasted_iota(jnp.int32, (BLK, BLK), 1)

    def static_sign(a, b):
        return 1.0 - 2.0 * (bin(a & b).count("1") & 1)

    @pl.loop(0, ib)
    def _(k):
        for g in range(groups):
            signs = si_ref[k, :, g * BLK : (g + 1) * BLK].astype(jnp.float32)
            scaled = jnp.where(diagonal, signs, 0.0).astype(jnp.bfloat16)
            skin[k, g * BLK : (g + 1) * BLK, :] = jnp.dot(
                scaled, table_b, preferred_element_type=jnp.float32
            ).astype(jnp.bfloat16)

    @pl.loop(0, ob)
    def _(j):
        for g in range(groups):
            signs = so_ref[j, :, g * BLK : (g + 1) * BLK].astype(jnp.float32)
            plus = (table * signs).astype(jnp.bfloat16)
            minus = (table * -signs).astype(jnp.bfloat16)
            for h in range(groups):
                kout[j, h * BLK : (h + 1) * BLK, g * BLK : (g + 1) * BLK] = plus if static_sign(g, h) > 0 else minus

    def inner(t, slot):
        for g in range(groups):
            parity = 0
            for bit in bits_of(groups):
                if g & bit:
                    parity = parity + lax.rem(t // bit, 2)
            sign = (1 - 2 * lax.rem(parity + 0 * t, 2)).astype(jnp.float32)
            for k in range(ib):
                rows = slice(g * BLK, (g + 1) * BLK)
                kin[k, rows, :] = (skin[k, rows, :].astype(jnp.float32) * sign).astype(jnp.bfloat16)

        @pl.loop(0, ob)
        def _(j):
            @pl.loop(0, ib)
            def _(k):
                q = (t * ob + j) * ib + k
                w_copy(q).wait()

                @pl.when(q + WEIGHT_SLOTS - 1 < chunks * blocks)
                def _():
                    w_copy(q + WEIGHT_SLOTS - 1).start()

                wslot = lax.rem(q, WEIGHT_SLOTS)

                @pl.loop(0, INNER // GROUP)
                def _(m):
                    rows = pl.ds(pl.multiple_of(m * GROUP, GROUP), GROUP)
                    cols = pl.ds(pl.multiple_of(k * BLK, BLK), BLK)
                    right[rows, cols] = jnp.dot(
                        wbuf[wslot, rows, :], kin[k], preferred_element_type=jnp.float32
                    ).astype(jnp.bfloat16)

            @pl.loop(0, INNER // GROUP)
            def _(m):
                rows = pl.ds(pl.multiple_of(m * GROUP, GROUP), GROUP)
                both = jnp.dot(kout[j, rows, :], right[...], preferred_element_type=jnp.float32)
                per = GROUP // pr
                sbuf[slot, pl.ds(m * per, per), :, j] = both.reshape(per, S, ds, wide).astype(jnp.bfloat16)

    def send(t, slot):
        @pl.loop(0, S)
        def _(s):
            u = t * S + s
            pltpu.make_async_copy(sbuf.at[slot, me, s], recv_ref.at[u, me], own_sem.at[slot]).start()

            @pl.loop(1, n)
            def _(i):
                target, place = peer(n - i)
                pltpu.make_async_remote_copy(
                    src_ref=sbuf.at[slot, place, s], dst_ref=recv_ref.at[u, me],
                    send_sem=ssem.at[slot], recv_sem=rsem.at[u],
                    device_id=target, device_id_type=MESH,
                ).start()

    def wait_send(slot):
        sent = sbuf.at[slot, pl.ds(0, n - 1)]
        pltpu.make_async_copy(sent, sent, ssem.at[slot]).wait()
        own = sbuf.at[slot, me]
        pltpu.make_async_copy(own, own, own_sem.at[slot]).wait()

    d_block = me * pr // BLK
    d_blocks = INNER // BLK

    def read_levels():
        pltpu.make_async_copy(levv, levv, lev_recv).wait()
        level = levv[...].astype(jnp.float32).reshape(n * ob, d_blocks, lev_cols)
        line = lax.broadcasted_iota(jnp.int32, level.shape, 1)
        level = jnp.sum(jnp.where(line == d_block, level, 0.0), axis=1, keepdims=True)
        level = jnp.broadcast_to(level, (n * ob, d_blocks, lev_cols)).reshape(n * ob * d_blocks, lev_cols)
        levb[...] = level.astype(jnp.bfloat16)

    def outer(t):
        lane = lax.broadcasted_iota(jnp.int32, (lev_cols, wide), 1)
        line = lax.broadcasted_iota(jnp.int32, (lev_cols, wide), 0)
        pick = jnp.where(line == (lane >> 7) * d_blocks + t, float(D // LEVEL_UNIT), 0.0).astype(jnp.bfloat16)
        lim[...] = jnp.dot(levb[...], pick, preferred_element_type=jnp.float32).reshape(lim.shape)

        @pl.loop(0, S)
        def _(s):
            u = t * S + s
            arrived = recv_ref.at[u, pl.ds(0, n - 1)]
            pltpu.make_async_copy(arrived, arrived, rsem.at[u]).wait()
            fetch = pltpu.make_async_copy(recv_ref.at[u], rbuf, usem)
            fetch.start()
            fetch.wait()

            @pl.loop(0, ai)
            def _(i):
                cc, k = i // ib, lax.rem(i, ib)
                cols = pl.ds(pl.multiple_of(k * BLK, BLK), BLK)
                mixed = butterfly(
                    rbuf[rr * C + cc, j, :, cols].astype(jnp.float32) for rr in range(R) for j in range(ob)
                )
                for o in range(ao):
                    mix[i, o] = mixed[o]

            @pl.loop(0, ao)
            def _(o):
                rr, j = o // ob, lax.rem(o, ob)
                mixed = butterfly(mix[i, o] for i in range(ai))
                for i in range(ai):
                    cc, k = i // ib, i % ib
                    limit = lim[(rr * C + cc) * ob + j, :, k * BLK : (k + 1) * BLK]
                    value = mixed[i].reshape(ds // d_blocks, d_blocks, BLK)
                    value = jnp.minimum(jnp.maximum(value, -limit), limit)
                    clip[i, o] = value.reshape(ds, BLK).astype(jnp.bfloat16)

            total = None
            for i in range(ai):
                cc, k = i // ib, i % ib
                cols = pl.ds(pl.multiple_of(k * INNER + t * BLK, BLK), BLK)
                cal = jnp.concatenate([calv[cal_slot(rr, cc), :, cols] for rr in range(R)], axis=0)
                term = lax.dot_general(
                    cal, clip[i].reshape(ao * ds, BLK), (((1,), (1,)), ((), ())), preferred_element_type=jnp.float32
                )
                total = term if total is None else total + term
            acc[s] += total

    spot = lax.broadcasted_iota(jnp.int32, perm.shape[1:], 0)
    lane = lax.broadcasted_iota(jnp.int32, perm.shape[1:], 1)
    shift = pr.bit_length() - 1
    step = ds.bit_length() - 1
    for q in range(R):
        for s in range(S):
            wanted = (q * ob + (lane >> shift)) * ds + (lane & (ds - 1))
            hit = (spot == wanted) & (((lane & (pr - 1)) >> step) == s)
            perm[q * S + s] = jnp.where(hit, 1.0, 0.0).astype(jnp.bfloat16)
    acc[...] = jnp.zeros_like(acc)

    @pl.loop(0, chunks + SEND_SLOTS)
    def _(i):
        slot = lax.rem(i, SEND_SLOTS)

        @pl.when(i >= SEND_SLOTS)
        def _():
            wait_send(slot)

        @pl.when(i < chunks)
        def _():
            inner(i, slot)
            send(i, slot)

        for at in range(SEND_SLOTS + 1):
            @pl.when(i == at)
            def _():
                cal_advance(at)
                if at == SEND_SLOTS:
                    for later in range(at + 1, stages):
                        cal_advance(later)
                    read_levels()

        @pl.when(i >= SEND_SLOTS)
        def _():
            outer(i - SEND_SLOTS)

    accb[...] = (acc[...] * (1.0 / D)).astype(jnp.bfloat16)
    rows_each = ostage.shape[1]

    @pl.loop(0, R)
    def _(q):
        total = None
        for s in range(S):
            term = jnp.dot(accb[s], perm[q * S + s], preferred_element_type=jnp.float32)
            total = term if total is None else total + term
        for cc in range(C):
            ostage[q * C + cc] = total[cc * rows_each : (cc + 1) * rows_each].astype(jnp.bfloat16)

    pltpu.make_async_copy(ostage.at[me], out_ref.at[me], out_recv).start()

    @pl.loop(1, n)
    def _(i):
        target, place = peer(n - i)
        pltpu.make_async_remote_copy(
            src_ref=ostage.at[place], dst_ref=out_ref.at[me], send_sem=out_send, recv_sem=out_recv,
            device_id=target, device_id_type=MESH,
        ).start()

    for stage in range(stages):
        cal_copy(stage).wait_send()
    sent = levv.at[pl.ds(0, n - 1)]
    pltpu.make_async_copy(sent, sent, lev_send).wait()
    pltpu.make_async_copy(out_ref, out_ref, out_recv).wait()
    sent = ostage.at[pl.ds(0, n - 1)]
    pltpu.make_async_copy(sent, sent, out_send).wait()


def shards(query_weight, sign_input, sign_output, clip_level, calibration):
    rows_local, cols_local = query_weight.shape
    R, C = lax.axis_size("row"), lax.axis_size("col")
    n = R * C
    ob, ib = rows_local // INNER, cols_local // INNER
    pr = INNER // n
    ds = min(16, pr)
    S = pr // ds
    chunks = INNER // BLK
    cal_local = calibration.shape[0]
    cal_rows = R * cal_local
    ao, ai = R * ob, C * ib
    wide = ib * BLK
    stages = len(bits_of(R)) + len(bits_of(C))
    bf16, f32 = jnp.bfloat16, jnp.float32

    _, result = pl.pallas_call(
        functools.partial(kernel, R, C),
        in_specs=[
            pl.BlockSpec(memory_space=pl.ANY),
            pl.BlockSpec(memory_space=pltpu.VMEM),
            pl.BlockSpec(memory_space=pltpu.VMEM),
            pl.BlockSpec(memory_space=pl.ANY),
            pl.BlockSpec(memory_space=pl.ANY),
        ],
        out_specs=[pl.BlockSpec(memory_space=pl.ANY)] * 2,
        out_shape=[
            jax.ShapeDtypeStruct((chunks * S, n, ob, ds, wide), bf16),
            jax.ShapeDtypeStruct((n, cal_rows // C, ob * pr), bf16),
        ],
        scratch_shapes=[
            pltpu.VMEM((ob, INNER, INNER), bf16),
            pltpu.VMEM((ib, INNER, BLK), bf16),
            pltpu.VMEM((ib, INNER, BLK), bf16),
            pltpu.VMEM((WEIGHT_SLOTS, INNER, INNER), bf16),
            pltpu.VMEM((INNER, wide), bf16),
            pltpu.VMEM((SEND_SLOTS, n, S, ob, ds, wide), bf16),
            pltpu.VMEM((n, ob, ds, wide), bf16),
            pltpu.VMEM((ai, ao, ds, BLK), f32),
            pltpu.VMEM((ai, ao, ds, BLK), bf16),
            pltpu.VMEM((S, cal_rows, ao * ds), f32),
            pltpu.VMEM((S, cal_rows, ao * ds), bf16),
            pltpu.VMEM((R * S, ao * ds, ob * pr), bf16),
            pltpu.VMEM((n, cal_local, cols_local), bf16),
            pltpu.VMEM((n,) + clip_level.shape, jnp.int32),
            pltpu.VMEM((n * clip_level.shape[0], clip_level.shape[1]), bf16),
            pltpu.VMEM((n * ob, INNER // BLK, wide), f32),
            pltpu.VMEM((n, cal_rows // C, ob * pr), bf16),
            pltpu.SemaphoreType.DMA((WEIGHT_SLOTS,)),
            pltpu.SemaphoreType.DMA((SEND_SLOTS,)),
            pltpu.SemaphoreType.DMA((SEND_SLOTS,)),
            pltpu.SemaphoreType.DMA((chunks * S,)),
            pltpu.SemaphoreType.DMA,
            pltpu.SemaphoreType.DMA,
            pltpu.SemaphoreType.DMA((max(stages, 1),)),
            pltpu.SemaphoreType.DMA((max(stages, 1),)),
            pltpu.SemaphoreType.DMA,
            pltpu.SemaphoreType.DMA,
            pltpu.SemaphoreType.DMA,
            pltpu.SemaphoreType.DMA,
        ],
        compiler_params=pltpu.CompilerParams(
            collective_id=0, has_side_effects=True, vmem_limit_bytes=60 * 2**20
        ),
    )(query_weight, sign_input.reshape(ib, 1, INNER), sign_output.reshape(ob, 1, INNER), clip_level, calibration)

    result = result.reshape(n, cal_rows // C, ob, pr)
    return result.transpose(1, 2, 0, 3).reshape(cal_rows // C, rows_local)


def solution(mesh):
    placed = (
        P(("layer", "row"), "col"),
        P(("layer", "col")),
        P(("layer", "row")),
        P(("layer", "row"), "col"),
        P(("layer", "row"), "col"),
    )
    return jax.shard_map(
        shards, mesh=mesh, in_specs=placed, out_specs=P(("layer", "col"), "row"), check_vma=False
    )
```

time: 998 us -> 803 us (0.80)
  Pallas kernels: 238 us -> 799 us
  waiting for transfers between devices: 398 us -> 0 us
  blocking collectives: 219 us -> 0 us
  starting transfers between devices: 117 us -> 0 us
  between operations: 13.5 us -> 0.02 us
    pallas_call x5 -> x1, Pallas kernels: 238 us -> 799 us  [shards(): pl.pallas_call(functools.partial(kernel, R, C), in_specs=[pl.BlockSpec(me...]
    all_to_all x4 -> x0, waiting for transfers between devices: 398 us -> none  [shards(): lax.all_to_all(tile, axes, split_axis=0, concat_axis=0, tiled=True)]
    all_gather x2 -> x0, blocking collectives: 189 us -> none  [the longest x1 151 us: shards(): lax.all_gather(lax.all_gather(clip_level, 'col', axis=1, tiled=True), 'ro...]
    all_to_all x4 -> x0, starting transfers between devices: 117 us -> none  [shards(): lax.all_to_all(tile, axes, split_axis=0, concat_axis=0, tiled=True)]
    all_to_all x1 -> x0, blocking collectives: 29.3 us -> none  [shards(): lax.all_to_all(result, axes, split_axis=0, concat_axis=0, tiled=True)]
  transfers between devices with their start and end apart: 5 -> 0, of which waited for: 3 -> 0; matrix products, arithmetic and copies ran while one was open for 0% -> 0% of each run, Pallas kernels for 13% -> 0%
where the time goes in v1:
time: 803 us; the launch traced here: 802 us
  Pallas kernels  799 us (100%)
    pallas_call x1, Pallas kernels, shards(): pl.pallas_call(functools.partial(kernel, R, C), in_specs=[pl.BlockSpec(me...  799 us

profile of v1, /device:TPU:0, one launch (start us, length us, event | category | flops | bytes accessed | tf_op | source)
XLA Modules:
  0.0 801.7 jit_solution(5250760383505535573)
XLA Ops:
  0.0 798.8 %shard_map.55 = (bf16[32,16,4,16,512]{4,3,2,1,0:T(8,128)(2,1)}, bf16[16,96,256]{2,1,0:T(8,128)(2,1)}) custom-call(bf16[4096,4096]{1,0:T(8,128)(2,1)} %w_ref.1, s32[4,1,1024]{2,1,0:T(1,128)} %bitcast.8, s32[4,1,1024]{2,1,0:T(1,128)} %bitcast.9, s32[32,32]{1,0:T(8,128)} %level_ref.1, bf16[96,4096]{1,0:T(8,128)(2,1)} %cal_ref.1), custom_call_target="tpu_custom_call" | custom-call | tf_op jit(solution)/shard_map/pallas_call | solution.py:376
  798.8 1.6 copy.7
  800.4 0.1 copy.8
  800.4 1.2 copy.9

commit v2 on v1

--- a/solution.py
+++ b/solution.py
@@ -228,6 +228,8 @@
     def wait_send(slot):
         sent = sbuf.at[slot, pl.ds(0, n - 1)]
         pltpu.make_async_copy(sent, sent, ssem.at[slot]).wait()
+
+    def wait_own(slot):
         own = sbuf.at[slot, me]
         pltpu.make_async_copy(own, own, own_sem.at[slot]).wait()
 
@@ -306,10 +308,14 @@
 
         @pl.when(i >= SEND_SLOTS)
         def _():
-            wait_send(slot)
+            wait_own(slot)
 
         @pl.when(i < chunks)
         def _():
+            @pl.when(i >= SEND_SLOTS)
+            def _():
+                wait_send(slot)
+
             inner(i, slot)
             send(i, slot)
 
@@ -348,6 +354,8 @@
             device_id=target, device_id_type=MESH,
         ).start()
 
+    for t in range(chunks - SEND_SLOTS, chunks):
+        wait_send(t % SEND_SLOTS)
     for stage in range(stages):
         cal_copy(stage).wait_send()
     sent = levv.at[pl.ds(0, n - 1)]

time: 803 us -> 796 us (level)
  no operation moved by 1% of the time
where the time goes in v2:
time: 796 us; the launch traced here: 795 us
  Pallas kernels  792 us (99%)
    pallas_call x1, Pallas kernels, shards(): pl.pallas_call(functools.partial(kernel, R, C), in_specs=[pl.BlockSpec(me...  792 us

profile of v2, /device:TPU:0, one launch (start us, length us, event | category | flops | bytes accessed | tf_op | source)
XLA Modules:
  0.0 795.1 jit_solution(17351906120073198526)
XLA Ops:
  0.0 792.1 %shard_map.55 = (bf16[32,16,4,16,512]{4,3,2,1,0:T(8,128)(2,1)}, bf16[16,96,256]{2,1,0:T(8,128)(2,1)}) custom-call(bf16[4096,4096]{1,0:T(8,128)(2,1)} %w_ref.1, s32[4,1,1024]{2,1,0:T(1,128)} %bitcast.8, s32[4,1,1024]{2,1,0:T(1,128)} %bitcast.9, s32[32,32]{1,0:T(8,128)} %level_ref.1, bf16[96,4096]{1,0:T(8,128)(2,1)} %cal_ref.1), custom_call_target="tpu_custom_call" | custom-call | tf_op jit(solution)/shard_map/pallas_call | solution.py:384
  792.1 1.6 copy.7
  793.7 0.1 copy.8
  793.8 1.2 copy.9

commit v3 on v2

--- a/solution.py
+++ b/solution.py
@@ -23,6 +23,10 @@
         size //= 2
         bits.append(size)
     return bits
+
+
+def mixed_order(n, i):
+    return n // 2 * lax.rem(i, 2) + i // 2
 
 
 def flip(at, bit):
@@ -218,7 +222,7 @@
 
             @pl.loop(1, n)
             def _(i):
-                target, place = peer(n - i)
+                target, place = peer(mixed_order(n, i))
                 pltpu.make_async_remote_copy(
                     src_ref=sbuf.at[slot, place, s], dst_ref=recv_ref.at[u, me],
                     send_sem=ssem.at[slot], recv_sem=rsem.at[u],

time: 796 us -> 794 us (level)
  no operation moved by 1% of the time
where the time goes in v3:
time: 794 us; the launch traced here: 792 us
  Pallas kernels  789 us (99%)
    pallas_call x1, Pallas kernels, shards(): pl.pallas_call(functools.partial(kernel, R, C), in_specs=[pl.BlockSpec(me...  789 us

profile of v3, /device:TPU:0, one launch (start us, length us, event | category | flops | bytes accessed | tf_op | source)
XLA Modules:
  0.0 792.1 jit_solution(5765297377167748822)
XLA Ops:
  0.0 789.1 %shard_map.55 = (bf16[32,16,4,16,512]{4,3,2,1,0:T(8,128)(2,1)}, bf16[16,96,256]{2,1,0:T(8,128)(2,1)}) custom-call(bf16[4096,4096]{1,0:T(8,128)(2,1)} %w_ref.1, s32[4,1,1024]{2,1,0:T(1,128)} %bitcast.8, s32[4,1,1024]{2,1,0:T(1,128)} %bitcast.9, s32[32,32]{1,0:T(8,128)} %level_ref.1, bf16[96,4096]{1,0:T(8,128)(2,1)} %cal_ref.1), custom_call_target="tpu_custom_call" | custom-call | tf_op jit(solution)/shard_map/pallas_call | solution.py:388
  789.1 1.6 copy.7
  790.7 0.1 copy.8
  790.8 1.2 copy.9

commit v4 on v3

--- a/solution.py
+++ b/solution.py
@@ -61,9 +61,9 @@
 
 
 def kernel(
-    R, C, w_ref, si_ref, so_ref, level_ref, cal_ref, recv_ref, out_ref,
-    kout, skin, kin, wbuf, right, sbuf, rbuf, mix, clip, acc, accb, perm, calv, levv, levb, lim, ostage,
-    wsem, ssem, own_sem, rsem, usem, cal_own, cal_send, cal_recv, lev_send, lev_recv, out_send, out_recv,
+    R, C, w_ref, si_hbm, so_hbm, level_ref, cal_ref, recv_ref, out_ref,
+    si_ref, so_ref, kout, skin, kin, wbuf, right, sbuf, rbuf, mix, clip, acc, accb, perm, calv, levv, levb, lim, ostage,
+    sign_sem, wsem, ssem, own_sem, rsem, usem, cal_own, cal_send, cal_recv, lev_send, lev_recv, out_send, out_recv,
 ):
     layer, r, c = lax.axis_index("layer"), lax.axis_index("row"), lax.axis_index("col")
     n = R * C
@@ -72,6 +72,8 @@
     ib = wide // BLK
     chunks = INNER // BLK
     S = units // chunks
+    H = out_ref.shape[0]
+    last = chunks - 1
     pr = S * ds
     ao, ai = R * ob, C * ib
     groups = INNER // BLK
@@ -133,6 +135,12 @@
         target, _ = peer(i)
         pl.semaphore_signal(barrier, inc=1, device_id=target, device_id_type=MESH)
 
+    sign_copies = [
+        pltpu.make_async_copy(si_hbm, si_ref, sign_sem.at[0]),
+        pltpu.make_async_copy(so_hbm, so_ref, sign_sem.at[1]),
+    ]
+    for copy in sign_copies:
+        copy.start()
     cal_own_copy.start()
     for q in range(WEIGHT_SLOTS - 1):
         w_copy(q).start()
@@ -153,6 +161,9 @@
     table = sylvester(BLK)
     table_b = table.astype(jnp.bfloat16)
     diagonal = lax.broadcasted_iota(jnp.int32, (BLK, BLK), 0) == lax.broadcasted_iota(jnp.int32, (BLK, BLK), 1)
+
+    for copy in sign_copies:
+        copy.wait()
 
     def static_sign(a, b):
         return 1.0 - 2.0 * (bin(a & b).count("1") & 1)
@@ -248,6 +259,33 @@
         level = jnp.broadcast_to(level, (n * ob, d_blocks, lev_cols)).reshape(n * ob * d_blocks, lev_cols)
         levb[...] = level.astype(jnp.bfloat16)
 
+    def finish(h):
+        own_units = range(h * (S // H), (h + 1) * (S // H))
+        rows_each = ostage.shape[2]
+        for s in own_units:
+            accb[s] = (acc[s] * (1.0 / D)).astype(jnp.bfloat16)
+
+        @pl.loop(0, R)
+        def _(q):
+            total = None
+            for s in own_units:
+                term = jnp.dot(accb[s], perm[q * S + s], preferred_element_type=jnp.float32)
+                total = term if total is None else total + term
+            for cc in range(C):
+                ostage[h, q * C + cc] = total[cc * rows_each : (cc + 1) * rows_each].astype(jnp.bfloat16)
+
+    def send_out(h):
+        pltpu.make_async_copy(ostage.at[h, me], out_ref.at[h, me], out_recv.at[h]).start()
+
+        @pl.loop(1, n)
+        def _(i):
+            target, place = peer(n - i)
+            pltpu.make_async_remote_copy(
+                src_ref=ostage.at[h, place], dst_ref=out_ref.at[h, me],
+                send_sem=out_send.at[h], recv_sem=out_recv.at[h],
+                device_id=target, device_id_type=MESH,
+            ).start()
+
     def outer(t):
         lane = lax.broadcasted_iota(jnp.int32, (lev_cols, wide), 1)
         line = lax.broadcasted_iota(jnp.int32, (lev_cols, wide), 0)
@@ -257,8 +295,19 @@
         @pl.loop(0, S)
         def _(s):
             u = t * S + s
+            final_unit = (t == last) & (s == S - 1)
+            if H > 1:
+                @pl.when(final_unit)
+                def _():
+                    finish(0)
+
             arrived = recv_ref.at[u, pl.ds(0, n - 1)]
             pltpu.make_async_copy(arrived, arrived, rsem.at[u]).wait()
+            if H > 1:
+                @pl.when(final_unit)
+                def _():
+                    send_out(0)
+
             fetch = pltpu.make_async_copy(recv_ref.at[u], rbuf, usem)
             fetch.start()
             fetch.wait()
@@ -297,12 +346,12 @@
 
     spot = lax.broadcasted_iota(jnp.int32, perm.shape[1:], 0)
     lane = lax.broadcasted_iota(jnp.int32, perm.shape[1:], 1)
-    shift = pr.bit_length() - 1
+    shift = (pr // H).bit_length() - 1
     step = ds.bit_length() - 1
     for q in range(R):
         for s in range(S):
             wanted = (q * ob + (lane >> shift)) * ds + (lane & (ds - 1))
-            hit = (spot == wanted) & (((lane & (pr - 1)) >> step) == s)
+            hit = (spot == wanted) & (((lane & (pr // H - 1)) >> step) == s % (S // H))
             perm[q * S + s] = jnp.where(hit, 1.0, 0.0).astype(jnp.bfloat16)
     acc[...] = jnp.zeros_like(acc)
 
@@ -336,27 +385,8 @@
         def _():
             outer(i - SEND_SLOTS)
 
-    accb[...] = (acc[...] * (1.0 / D)).astype(jnp.bfloat16)
-    rows_each = ostage.shape[1]
-
-    @pl.loop(0, R)
-    def _(q):
-        total = None
-        for s in range(S):
-            term = jnp.dot(accb[s], perm[q * S + s], preferred_element_type=jnp.float32)
-            total = term if total is None else total + term
-        for cc in range(C):
-            ostage[q * C + cc] = total[cc * rows_each : (cc + 1) * rows_each].astype(jnp.bfloat16)
-
-    pltpu.make_async_copy(ostage.at[me], out_ref.at[me], out_recv).start()
-
-    @pl.loop(1, n)
-    def _(i):
-        target, place = peer(n - i)
-        pltpu.make_async_remote_copy(
-            src_ref=ostage.at[place], dst_ref=out_ref.at[me], send_sem=out_send, recv_sem=out_recv,
-            device_id=target, device_id_type=MESH,
-        ).start()
+    finish(H - 1)
+    send_out(H - 1)
 
     for t in range(chunks - SEND_SLOTS, chunks):
         wait_send(t % SEND_SLOTS)
@@ -364,9 +394,10 @@
         cal_copy(stage).wait_send()
     sent = levv.at[pl.ds(0, n - 1)]
     pltpu.make_async_copy(sent, sent, lev_send).wait()
-    pltpu.make_async_copy(out_ref, out_ref, out_recv).wait()
-    sent = ostage.at[pl.ds(0, n - 1)]
-    pltpu.make_async_copy(sent, sent, out_send).wait()
+    for h in range(H):
+        pltpu.make_async_copy(out_ref.at[h], out_ref.at[h], out_recv.at[h]).wait()
+        sent = ostage.at[h, pl.ds(0, n - 1)]
+        pltpu.make_async_copy(sent, sent, out_send.at[h]).wait()
 
 
 def shards(query_weight, sign_input, sign_output, clip_level, calibration):
@@ -377,6 +408,7 @@
     pr = INNER // n
     ds = min(16, pr)
     S = pr // ds
+    H = 2 if S % 2 == 0 else 1
     chunks = INNER // BLK
     cal_local = calibration.shape[0]
     cal_rows = R * cal_local
@@ -389,17 +421,19 @@
         functools.partial(kernel, R, C),
         in_specs=[
             pl.BlockSpec(memory_space=pl.ANY),
-            pl.BlockSpec(memory_space=pltpu.VMEM),
-            pl.BlockSpec(memory_space=pltpu.VMEM),
+            pl.BlockSpec(memory_space=pl.ANY),
+            pl.BlockSpec(memory_space=pl.ANY),
             pl.BlockSpec(memory_space=pl.ANY),
             pl.BlockSpec(memory_space=pl.ANY),
         ],
         out_specs=[pl.BlockSpec(memory_space=pl.ANY)] * 2,
         out_shape=[
             jax.ShapeDtypeStruct((chunks * S, n, ob, ds, wide), bf16),
-            jax.ShapeDtypeStruct((n, cal_rows // C, ob * pr), bf16),
+            jax.ShapeDtypeStruct((H, n, cal_rows // C, ob * pr // H), bf16),
         ],
         scratch_shapes=[
+            pltpu.VMEM((ib, 1, INNER), jnp.int32),
+            pltpu.VMEM((ob, 1, INNER), jnp.int32),
             pltpu.VMEM((ob, INNER, INNER), bf16),
             pltpu.VMEM((ib, INNER, BLK), bf16),
             pltpu.VMEM((ib, INNER, BLK), bf16),
@@ -411,12 +445,13 @@
             pltpu.VMEM((ai, ao, ds, BLK), bf16),
             pltpu.VMEM((S, cal_rows, ao * ds), f32),
             pltpu.VMEM((S, cal_rows, ao * ds), bf16),
-            pltpu.VMEM((R * S, ao * ds, ob * pr), bf16),
+            pltpu.VMEM((R * S, ao * ds, ob * pr // H), bf16),
             pltpu.VMEM((n, cal_local, cols_local), bf16),
             pltpu.VMEM((n,) + clip_level.shape, jnp.int32),
             pltpu.VMEM((n * clip_level.shape[0], clip_level.shape[1]), bf16),
             pltpu.VMEM((n * ob, INNER // BLK, wide), f32),
-            pltpu.VMEM((n, cal_rows // C, ob * pr), bf16),
+            pltpu.VMEM((H, n, cal_rows // C, ob * pr // H), bf16),
+            pltpu.SemaphoreType.DMA((2,)),
             pltpu.SemaphoreType.DMA((WEIGHT_SLOTS,)),
             pltpu.SemaphoreType.DMA((SEND_SLOTS,)),
             pltpu.SemaphoreType.DMA((SEND_SLOTS,)),
@@ -427,16 +462,16 @@
             pltpu.SemaphoreType.DMA((max(stages, 1),)),
             pltpu.SemaphoreType.DMA,
             pltpu.SemaphoreType.DMA,
-            pltpu.SemaphoreType.DMA,
-            pltpu.SemaphoreType.DMA,
+            pltpu.SemaphoreType.DMA((H,)),
+            pltpu.SemaphoreType.DMA((H,)),
         ],
         compiler_params=pltpu.CompilerParams(
             collective_id=0, has_side_effects=True, vmem_limit_bytes=60 * 2**20
         ),
     )(query_weight, sign_input.reshape(ib, 1, INNER), sign_output.reshape(ob, 1, INNER), clip_level, calibration)
 
-    result = result.reshape(n, cal_rows // C, ob, pr)
-    return result.transpose(1, 2, 0, 3).reshape(cal_rows // C, rows_local)
+    result = result.reshape(H, n, cal_rows // C, ob, pr // H)
+    return result.transpose(2, 3, 1, 0, 4).reshape(cal_rows // C, rows_local)
 
 
 def solution(mesh):

time: 794 us -> 792 us (level)
  no operation moved by 1% of the time
where the time goes in v4:
time: 792 us; the launch traced here: 791 us
  Pallas kernels  788 us (99%)
    pallas_call x1, Pallas kernels, shards(): pl.pallas_call(functools.partial(kernel, R, C), in_specs=[pl.BlockSpec(me...  788 us

profile of v4, /device:TPU:0, one launch (start us, length us, event | category | flops | bytes accessed | tf_op | source)
XLA Modules:
  0.0 790.9 jit_solution(12051621298522486370)
XLA Ops:
  0.0 787.9 %shard_map.55 = (bf16[32,16,4,16,512]{4,3,2,1,0:T(8,128)(2,1)}, bf16[2,16,96,128]{3,2,1,0:T(8,128)(2,1)}) custom-call(bf16[4096,4096]{1,0:T(8,128)(2,1)} %w_ref.1, s32[4,1,1024]{2,1,0:T(1,128)} %bitcast.8, s32[4,1,1024]{2,1,0:T(1,128)} %bitcast.9, s32[32,32]{1,0:T(8,128)} %level_ref.1, bf16[96,4096]{1,0:T(8,128)(2,1)} %cal_ref.1), custom_call_target="tpu_custom_call" | custom-call | tf_op jit(solution)/shard_map/pallas_call | solution.py:420
  788.0 1.6 copy.7
  789.5 0.1 copy.8
  789.7 1.2 copy.9

commit v5 on v4

--- a/solution.py
+++ b/solution.py
@@ -63,7 +63,7 @@
 def kernel(
     R, C, w_ref, si_hbm, so_hbm, level_ref, cal_ref, recv_ref, out_ref,
     si_ref, so_ref, kout, skin, kin, wbuf, right, sbuf, rbuf, mix, clip, acc, accb, perm, calv, levv, levb, lim, ostage,
-    sign_sem, wsem, ssem, own_sem, rsem, usem, cal_own, cal_send, cal_recv, lev_send, lev_recv, out_send, out_recv,
+    sign_sem, wsem, ssem, own_sem, rsem, usem, cal_own, cal_send, cal_recv, lev_own, lev_send, lev_recv, out_send, out_recv,
 ):
     layer, r, c = lax.axis_index("layer"), lax.axis_index("row"), lax.axis_index("col")
     n = R * C
@@ -92,7 +92,7 @@
         cols = pl.ds(pl.multiple_of(lax.rem(block, ib) * INNER, INNER), INNER)
         return pltpu.make_async_copy(w_ref.at[rows, cols], wbuf.at[slot], wsem.at[slot])
 
-    def cal_slot(rr, cc):
+    def held_slot(rr, cc):
         slot, weight = 0, 1
         for bit in row_bits:
             slot = slot + weight * lax.rem(r // bit + rr // bit, 2)
@@ -102,31 +102,43 @@
             weight *= 2
         return slot
 
-    def cal_copy(stage):
+    def spread(stage, held, own_ref, send_sem, recv_sem):
         size = 2**stage
         if stage < len(row_bits):
             target = (layer, flip(r, row_bits[stage]), c)
         else:
             target = (layer, r, flip(c, col_bits[stage - len(row_bits)]))
         return pltpu.make_async_remote_copy(
-            src_ref=cal_ref if stage == 0 else calv.at[pl.ds(0, size)],
-            dst_ref=calv.at[1] if stage == 0 else calv.at[pl.ds(size, size)],
-            send_sem=cal_send.at[stage],
-            recv_sem=cal_recv.at[stage],
+            src_ref=own_ref if stage == 0 else held.at[pl.ds(0, size)],
+            dst_ref=held.at[1] if stage == 0 else held.at[pl.ds(size, size)],
+            send_sem=send_sem.at[stage],
+            recv_sem=recv_sem.at[stage],
             device_id=target,
             device_id_type=MESH,
         )
 
-    cal_own_copy = pltpu.make_async_copy(cal_ref, calv.at[0], cal_own)
-
-    def cal_advance(stage):
+    def stage_copies(stage):
+        return (
+            spread(stage, levv, level_ref, lev_send, lev_recv),
+            spread(stage, calv, cal_ref, cal_send, cal_recv),
+        )
+
+    own_copies = (
+        pltpu.make_async_copy(level_ref, levv.at[0], lev_own),
+        pltpu.make_async_copy(cal_ref, calv.at[0], cal_own),
+    )
+
+    def advance(stage):
         if stage >= stages:
             return
         if stage == 0:
-            cal_own_copy.wait()
-        cal_copy(stage).wait_recv()
+            for copy in own_copies:
+                copy.wait()
+        for copy in stage_copies(stage):
+            copy.wait_recv()
         if stage + 1 < stages:
-            cal_copy(stage + 1).start()
+            for copy in stage_copies(stage + 1):
+                copy.start()
 
     barrier = pltpu.get_barrier_semaphore()
 
@@ -141,22 +153,15 @@
     ]
     for copy in sign_copies:
         copy.start()
-    cal_own_copy.start()
+    for copy in own_copies:
+        copy.start()
     for q in range(WEIGHT_SLOTS - 1):
         w_copy(q).start()
     pl.semaphore_wait(barrier, n - 1)
 
     if stages:
-        cal_copy(0).start()
-    pltpu.make_async_copy(level_ref, levv.at[me], lev_recv).start()
-
-    @pl.loop(1, n)
-    def _(i):
-        target, _ = peer(i)
-        pltpu.make_async_remote_copy(
-            src_ref=level_ref, dst_ref=levv.at[me], send_sem=lev_send, recv_sem=lev_recv,
-            device_id=target, device_id_type=MESH,
-        ).start()
+        for copy in stage_copies(0):
+            copy.start()
 
     table = sylvester(BLK)
     table_b = table.astype(jnp.bfloat16)
@@ -252,7 +257,6 @@
     d_blocks = INNER // BLK
 
     def read_levels():
-        pltpu.make_async_copy(levv, levv, lev_recv).wait()
         level = levv[...].astype(jnp.float32).reshape(n * ob, d_blocks, lev_cols)
         line = lax.broadcasted_iota(jnp.int32, level.shape, 1)
         level = jnp.sum(jnp.where(line == d_block, level, 0.0), axis=1, keepdims=True)
@@ -325,10 +329,11 @@
             @pl.loop(0, ao)
             def _(o):
                 rr, j = o // ob, lax.rem(o, ob)
+                slots = [held_slot(rr, cc) for cc in range(C)]
                 mixed = butterfly(mix[i, o] for i in range(ai))
                 for i in range(ai):
                     cc, k = i // ib, i % ib
-                    limit = lim[(rr * C + cc) * ob + j, :, k * BLK : (k + 1) * BLK]
+                    limit = lim[slots[cc] * ob + j, :, k * BLK : (k + 1) * BLK]
                     value = mixed[i].reshape(ds // d_blocks, d_blocks, BLK)
                     value = jnp.minimum(jnp.maximum(value, -limit), limit)
                     clip[i, o] = value.reshape(ds, BLK).astype(jnp.bfloat16)
@@ -337,7 +342,7 @@
             for i in range(ai):
                 cc, k = i // ib, i % ib
                 cols = pl.ds(pl.multiple_of(k * INNER + t * BLK, BLK), BLK)
-                cal = jnp.concatenate([calv[cal_slot(rr, cc), :, cols] for rr in range(R)], axis=0)
+                cal = jnp.concatenate([calv[held_slot(rr, cc), :, cols] for rr in range(R)], axis=0)
                 term = lax.dot_general(
                     cal, clip[i].reshape(ao * ds, BLK), (((1,), (1,)), ((), ())), preferred_element_type=jnp.float32
                 )
@@ -375,10 +380,10 @@
         for at in range(SEND_SLOTS + 1):
             @pl.when(i == at)
             def _():
-                cal_advance(at)
+                advance(at)
                 if at == SEND_SLOTS:
                     for later in range(at + 1, stages):
-                        cal_advance(later)
+                        advance(later)
                     read_levels()
 
         @pl.when(i >= SEND_SLOTS)
@@ -391,9 +396,8 @@
     for t in range(chunks - SEND_SLOTS, chunks):
         wait_send(t % SEND_SLOTS)
     for stage in range(stages):
-        cal_copy(stage).wait_send()
-    sent = levv.at[pl.ds(0, n - 1)]
-    pltpu.make_async_copy(sent, sent, lev_send).wait()
+        for copy in stage_copies(stage):
+            copy.wait_send()
     for h in range(H):
         pltpu.make_async_copy(out_ref.at[h], out_ref.at[h], out_recv.at[h]).wait()
         sent = ostage.at[h, pl.ds(0, n - 1)]
@@ -461,7 +465,8 @@
             pltpu.SemaphoreType.DMA((max(stages, 1),)),
             pltpu.SemaphoreType.DMA((max(stages, 1),)),
             pltpu.SemaphoreType.DMA,
-            pltpu.SemaphoreType.DMA,
+            pltpu.SemaphoreType.DMA((max(stages, 1),)),
+            pltpu.SemaphoreType.DMA((max(stages, 1),)),
             pltpu.SemaphoreType.DMA((H,)),
             pltpu.SemaphoreType.DMA((H,)),
         ],

time: 792 us -> 787 us (level)
  no operation moved by 1% of the time
where the time goes in v5:
time: 787 us; the launch traced here: 786 us
  Pallas kernels  783 us (99%)
    pallas_call x1, Pallas kernels, shards(): pl.pallas_call(functools.partial(kernel, R, C), in_specs=[pl.BlockSpec(me...  783 us

profile of v5, /device:TPU:0, one launch (start us, length us, event | category | flops | bytes accessed | tf_op | source)
XLA Modules:
  0.0 786.0 jit_solution(2116180922703468931)
XLA Ops:
  0.0 783.0 %shard_map.55 = (bf16[32,16,4,16,512]{4,3,2,1,0:T(8,128)(2,1)}, bf16[2,16,96,128]{3,2,1,0:T(8,128)(2,1)}) custom-call(bf16[4096,4096]{1,0:T(8,128)(2,1)} %w_ref.1, s32[4,1,1024]{2,1,0:T(1,128)} %bitcast.8, s32[4,1,1024]{2,1,0:T(1,128)} %bitcast.9, s32[32,32]{1,0:T(8,128)} %level_ref.1, bf16[96,4096]{1,0:T(8,128)(2,1)} %cal_ref.1), custom_call_target="tpu_custom_call" | custom-call | tf_op jit(solution)/shard_map/pallas_call | solution.py:424
  783.0 1.6 copy.7
  784.6 0.1 copy.8
  784.8 1.2 copy.9

commit v6 on v5

--- a/solution.py
+++ b/solution.py
@@ -355,7 +355,8 @@
     step = ds.bit_length() - 1
     for q in range(R):
         for s in range(S):
-            wanted = (q * ob + (lane >> shift)) * ds + (lane & (ds - 1))
+            turn = lax.rem(me, ob // H) * H + s // (S // H) if perm.shape[2] == BLK else 0
+            wanted = (q * ob + (((lane >> shift) + ob - turn) & (ob - 1))) * ds + (lane & (ds - 1))
             hit = (spot == wanted) & (((lane & (pr // H - 1)) >> step) == s % (S // H))
             perm[q * S + s] = jnp.where(hit, 1.0, 0.0).astype(jnp.bfloat16)
     acc[...] = jnp.zeros_like(acc)
@@ -402,6 +403,24 @@
         pltpu.make_async_copy(out_ref.at[h], out_ref.at[h], out_recv.at[h]).wait()
         sent = ostage.at[h, pl.ds(0, n - 1)]
         pltpu.make_async_copy(sent, sent, out_send.at[h]).wait()
+
+
+def merge_kernel(ob, x_ref, o_ref):
+    H, n, rows, _ = x_ref.shape
+    width = BLK // ob
+    joined = ob // H
+    tiles = n // joined
+    slot = lax.broadcasted_iota(jnp.int32, (rows, BLK), 1) // width
+    for at in range(tiles):
+        values = [x_ref[k % H, at * joined + k // H].astype(jnp.float32) for k in range(ob)]
+        for j in range(ob):
+            merged = values[0]
+            for k in range(1, ob):
+                merged = jnp.where(slot == (j + k) % ob, values[k], merged)
+            if j:
+                merged = pltpu.roll(merged, BLK - j * width, 1)
+            cols = slice((j * tiles + at) * BLK, (j * tiles + at + 1) * BLK)
+            o_ref[:, cols] = merged.astype(jnp.bfloat16)
 
 
 def shards(query_weight, sign_input, sign_output, clip_level, calibration):
@@ -475,8 +494,18 @@
         ),
     )(query_weight, sign_input.reshape(ib, 1, INNER), sign_output.reshape(ob, 1, INNER), clip_level, calibration)
 
-    result = result.reshape(H, n, cal_rows // C, ob, pr // H)
-    return result.transpose(2, 3, 1, 0, 4).reshape(cal_rows // C, rows_local)
+    rows_out = cal_rows // C
+    if ob * pr // H == BLK:
+        block = rows_out // 2 if rows_out % 32 == 0 else rows_out
+        return pl.pallas_call(
+            functools.partial(merge_kernel, ob),
+            grid=(rows_out // block,),
+            in_specs=[pl.BlockSpec((H, n, block, BLK), lambda i: (0, 0, i, 0))],
+            out_specs=pl.BlockSpec((block, rows_local), lambda i: (i, 0)),
+            out_shape=jax.ShapeDtypeStruct((rows_out, rows_local), bf16),
+        )(result)
+    result = result.reshape(H, n, rows_out, ob, pr // H)
+    return result.transpose(2, 3, 1, 0, 4).reshape(rows_out, rows_local)
 
 
 def solution(mesh):

time: 787 us -> 786 us (level)
  no operation moved by 1% of the time
where the time goes in v6:
time: 786 us; the launch traced here: 785 us
  Pallas kernels  785 us (100%)
    pallas_call x1, Pallas kernels, shards(): pl.pallas_call(functools.partial(kernel, R, C), in_specs=[pl.BlockSpec(me...  783 us

profile of v6, /device:TPU:0, one launch (start us, length us, event | category | flops | bytes accessed | tf_op | source)
XLA Modules:
  0.0 785.1 jit_solution(13124777870808582797)
XLA Ops:
  0.0 782.9 %shard_map.55 = (bf16[32,16,4,16,512]{4,3,2,1,0:T(8,128)(2,1)}, bf16[2,16,96,128]{3,2,1,0:T(8,128)(2,1)}) custom-call(bf16[4096,4096]{1,0:T(8,128)(2,1)} %w_ref.1, s32[4,1,1024]{2,1,0:T(1,128)} %bitcast.2, s32[4,1,1024]{2,1,0:T(1,128)} %bitcast.3, s32[32,32]{1,0:T(8,128)} %level_ref.1, bf16[96,4096]{1,0:T(8,128)(2,1)} %cal_ref.1), custom_call_target="tpu_custom_call" | custom-call | tf_op jit(solution)/shard_map/pallas_call | solution.py:443
  782.9 2.2 shard_map.56

commit v7 on v6

--- a/solution.py
+++ b/solution.py
@@ -283,7 +283,7 @@
 
         @pl.loop(1, n)
         def _(i):
-            target, place = peer(n - i)
+            target, place = peer(mixed_order(n, i))
             pltpu.make_async_remote_copy(
                 src_ref=ostage.at[h, place], dst_ref=out_ref.at[h, me],
                 send_sem=out_send.at[h], recv_sem=out_recv.at[h],

time: 786 us -> 785 us (level)
  no operation moved by 1% of the time
where the time goes in v7:
time: 785 us; the launch traced here: 783 us
  Pallas kernels  783 us (100%)
    pallas_call x1, Pallas kernels, shards(): pl.pallas_call(functools.partial(kernel, R, C), in_specs=[pl.BlockSpec(me...  781 us

profile of v7, /device:TPU:0, one launch (start us, length us, event | category | flops | bytes accessed | tf_op | source)
XLA Modules:
  0.0 783.4 jit_solution(4306384811011532097)
XLA Ops:
  0.0 781.2 %shard_map.55 = (bf16[32,16,4,16,512]{4,3,2,1,0:T(8,128)(2,1)}, bf16[2,16,96,128]{3,2,1,0:T(8,128)(2,1)}) custom-call(bf16[4096,4096]{1,0:T(8,128)(2,1)} %w_ref.1, s32[4,1,1024]{2,1,0:T(1,128)} %bitcast.2, s32[4,1,1024]{2,1,0:T(1,128)} %bitcast.3, s32[32,32]{1,0:T(8,128)} %level_ref.1, bf16[96,4096]{1,0:T(8,128)(2,1)} %cal_ref.1), custom_call_target="tpu_custom_call" | custom-call | tf_op jit(solution)/shard_map/pallas_call | solution.py:443
  781.2 2.2 shard_map.56
